TPU v7x, 256 devices: a whole 4x4x8 slice. The times are simulated.
256 devices in a mesh: row: 16 (over x, y), col: 16 (over z, core).
Axes of the slice: x: 4, y: 4, z: 8, core: 2. Of those that a mesh axis runs over, the one named last changes fastest.
Arguments:
- root_block: bfloat16 [16, 256, 4096], P('row', None, 'col'), may hold values from -1 to 3, as said below
- l_one: bfloat16 [16, 256, 4096], P('row', None, 'col'), may hold values from -0.09375 to 0.09375
- dinv_one: bfloat16 [16, 128, 4096], P('row', None, 'col'), may hold values from -1 to 3, as said below
- l_two: bfloat16 [16, 384, 4096], P('row', None, 'col'), may hold values from -0.078125 to 0.078125
- dinv_two: bfloat16 [16, 64, 4096], P('row', None, 'col'), may hold values from -1 to 3, as said below
- l_three: bfloat16 [16, 448, 4096], P('row', None, 'col'), may hold values from -0.0625 to 0.0625
- dinv_three: bfloat16 [16, 32, 4096], P('row', None, 'col'), may hold values from -1 to 3, as said below
Outputs:
- sigma_one: float32 [16, 384, 4096], P('row', None, 'col')
- sigma_two: float32 [16, 448, 4096], P('row', None, 'col')
- sigma_three: float32 [16, 480, 4096], P('row', None, 'col')
Inputs may be any that keep to these rules, and one draw needn't show every extreme that they name: Each node's diagonal block of root_block (in natural row order, in the node's columns) is exactly symmetric. `dinv_one`: each node's 2048 x 2048 block in natural row order is exactly symmetric. `dinv_two`: each node's 1024 x 1024 block in natural row order is exactly symmetric. `dinv_three`: each node's 512 x 512 block in natural row order is exactly symmetric.
All inputs are finite; a program needn't handle non-finite values.
Results may differ from a plain program's by a relative error of at most 0.0003.
Values may be sent and summed in bfloat16 or wider, within the bound.
A program may use at most 64 MiB of HBM per device.

v0:
```python
import jax
import jax.numpy as jnp
from jax import lax
from jax.sharding import PartitionSpec as P

S0 = 4096
S1 = 2048
S2 = 1024
S3 = 512
exact_mode = lax.Precision.HIGHEST


def swapped(value, axis, apart):
    mask = 2**apart
    pairs = [(source, source ^ mask) for source in range(lax.axis_size(axis))]
    return lax.ppermute(value, axis, pairs)


def product(left_side, right_side):
    return jnp.dot(left_side, right_side, precision=exact_mode, preferred_element_type=jnp.float32)


def transposed_product(left_side, right_side):
    return lax.dot_general(
        left_side,
        right_side,
        (((0,), (0,)), ((), ())),
        precision=exact_mode,
        preferred_element_type=jnp.float32,
    )


def doubling_order(own_tile, partner, position):
    column = lax.axis_index("col")
    higher = column // 2**position % 2 == 1
    return jnp.where(
        higher, jnp.concatenate([partner, own_tile], 1), jnp.concatenate([own_tile, partner], 1)
    )


def collect_panel(panel_tile, group_size):
    for position in range(group_size.bit_length() - 1):
        partner = swapped(panel_tile, "col", position)
        panel_tile = doubling_order(panel_tile, partner, position)
    return panel_tile


def per_device(root_block, l_one, dinv_one, l_two, dinv_two, l_three, dinv_three):
    run_count = lax.axis_size("row")
    tile_width = root_block.shape[2]
    block_widths = [S0, S1, S2, S3]
    run_rows = [block_width // run_count for block_width in block_widths]
    row_offsets = [
        0,
        run_rows[0],
        run_rows[0] + run_rows[1],
        run_rows[0] + run_rows[1] + run_rows[2],
    ]
    factors = [l_one[0], l_two[0], l_three[0]]
    inverses = [dinv_one[0], dinv_two[0], dinv_three[0]]
    root_rows = lax.all_gather(root_block[0], "col", axis=1, tiled=True)
    panels = [root_rows]
    crossed = [root_rows]
    outputs = []
    for tree_level in range(1, 4):
        factor_tile = factors[tree_level - 1]
        head_rows = row_offsets[tree_level]
        gathered = lax.all_gather(factor_tile, "row", axis=0, tiled=True)
        stacked = gathered.reshape(run_count, head_rows, tile_width)
        running = jnp.zeros((head_rows, tile_width), jnp.float32)
        for block_index in range(tree_level):
            natural_part = stacked[
                :, row_offsets[block_index] : row_offsets[block_index + 1], :
            ].reshape(block_widths[block_index], tile_width)
            if block_index == 0:
                term_rows = jnp.dot(panels[0], natural_part, preferred_element_type=jnp.float32)
            else:
                term_rows = product(panels[block_index], natural_part.astype(jnp.float32))
            running = running + jnp.pad(term_rows, ((0, head_rows - term_rows.shape[0]), (0, 0)))
        factor_float = factor_tile.astype(jnp.float32)
        if tree_level > 1:
            pieces = []
            for block_index in range(1, tree_level):
                partial_sum = transposed_product(
                    panels[block_index][: row_offsets[block_index]],
                    factor_float[: row_offsets[block_index]],
                )
                pieces.append(partial_sum.reshape(run_count, run_rows[block_index], tile_width))
            joined = jnp.concatenate(pieces, 1).reshape(
                run_count * (head_rows - row_offsets[1]), tile_width
            )
            reduced = lax.psum_scatter(joined, "row", scatter_dimension=0, tiled=True)
            running = running + jnp.pad(reduced, ((row_offsets[1], 0), (0, 0)))
        panel_rows = -running
        inverse_tile = inverses[tree_level - 1].astype(jnp.float32)
        group_size = block_widths[tree_level] // tile_width
        spread = collect_panel(panel_rows, group_size)
        diag_terms = transposed_product(spread, factor_float)
        diag_rows = inverse_tile - lax.psum_scatter(
            diag_terms, "row", scatter_dimension=0, tiled=True
        )
        sigma_tile = jnp.concatenate([panel_rows, diag_rows], 0)
        outputs.append(sigma_tile[None])
        if tree_level < 3:
            whole_panel = jnp.concatenate([spread, collect_panel(diag_rows, group_size)], 0)
            panels.append(whole_panel)
            crossed.append(whole_panel)
    return (outputs[0], outputs[1], outputs[2])


def solution(mesh):
    placed = (
        P("row", None, "col"),
        P("row", None, "col"),
        P("row", None, "col"),
        P("row", None, "col"),
        P("row", None, "col"),
        P("row", None, "col"),
        P("row", None, "col"),
    )
    return jax.shard_map(
        per_device,
        mesh=mesh,
        in_specs=placed,
        out_specs=(P("row", None, "col"), P("row", None, "col"), P("row", None, "col")),
        check_vma=False,
    )
```

profile of v0, /device:TPU:2, one launch (start us, length us, event | category | flops | bytes accessed | tf_op | source)
XLA Modules:
  0.0 705.2 jit_solution(9191428733446846489)
XLA Ops:
  8.7 45.0 %all-gather.9.cloned.1.call-done = bf16[1,256,4096]{2,1,0:T(8,128)(2,1)} async-done(((bf16[1,256,256]{2,1,0:T(8,128)(2,1)}), bf16[1,256,4096]{2,1,0:T(8,128)(2,1)}) %all-gather.9.cloned.1.call-update) | async-done | bytes 2097168 | tf_op jit(solution)/shard_map/all_gather | solution.py:61
  53.7 51.2 %all-gather.11.cloned.1.call-done = bf16[1,4096,256]{2,1,0:T(8,128)(2,1)} async-done(((bf16[1,256,256]{2,1,0:T(8,128)(2,1)}), bf16[1,4096,256]{2,1,0:T(8,128)(2,1)}) %all-gather.11.cloned.1.call-update) | async-done | bytes 2097168 | tf_op jit(solution)/shard_map/all_gather | solution.py:68
  104.9 3.1 fusion.25
  111.4 12.4 %collective-permute-done.1 = f32[256,512]{0,1:T(8,128)S(1)} collective-permute-done((f32[256,512]{0,1:T(8,128)S(1)}, f32[256,512]{0,1:T(8,128)S(1)}, u32[]{:S(2)}, u32[]{:S(2)}) %collective-permute-start.1) | collective-permute-done | bytes 524320 | tf_op jit(solution)/shard_map/ppermute | solution.py:16
  123.9 2.6 collective-permute-start.2
  126.5 45.3 %collective-permute-done.2 = f32[256,1024]{0,1:T(8,128)} collective-permute-done((f32[256,1024]{0,1:T(8,128)S(1)}, f32[256,1024]{0,1:T(8,128)}, u32[]{:S(2)}, u32[]{:S(2)}) %collective-permute-start.2) | collective-permute-done | bytes 1048608 | tf_op jit(solution)/shard_map/ppermute | solution.py:16
  173.7 2.6 fusion.47
  180.7 74.8 %reduce-scatter.6.cloned.1.call-done = f32[128,256]{0,1:T(8,128)} async-done(((f32[2048,256]{0,1:T(8,128)}), f32[128,256]{0,1:T(8,128)}) %reduce-scatter.6.cloned.1.call-update) | async-done | bytes 131088 | tf_op jit(solution)/shard_map/reduce_scatter | solution.py:99
  259.4 6.8 collective-permute-done.4
  266.3 2.6 collective-permute-start.5
  268.9 41.1 %all-gather.13.cloned.1.call-done = bf16[1,6144,256]{2,1,0:T(8,128)(2,1)} async-done(((bf16[1,384,256]{2,1,0:T(8,128)(2,1)}), bf16[1,6144,256]{2,1,0:T(8,128)(2,1)}) %all-gather.13.cloned.1.call-update) | async-done | bytes 3145744 | tf_op jit(solution)/shard_map/all_gather | solution.py:68
  317.3 75.3 %reduce-scatter.8.cloned.1.call-done = f32[128,256]{1,0:T(8,128)} async-done(((f32[2048,256]{1,0:T(8,128)}), f32[128,256]{1,0:T(8,128)}) %reduce-scatter.8.cloned.1.call-update) | async-done | bytes 131088 | tf_op jit(solution)/shard_map/reduce_scatter | solution.py:92
  392.6 4.2 fusion.24
  400.5 18.0 %collective-permute-done.7 = f32[384,512]{1,0:T(8,128)S(1)} collective-permute-done((f32[384,512]{1,0:T(8,128)S(1)}, f32[384,512]{1,0:T(8,128)S(1)}, u32[]{:S(2)}, u32[]{:S(2)}) %collective-permute-start.7) | collective-permute-done | bytes 786464 | tf_op jit(solution)/shard_map/ppermute | solution.py:16
  424.9 3.0 copy.16
  427.9 2.5 fusion.38
  432.5 16.3 %all-gather.15.cloned.1.call-done = bf16[1,7168,256]{2,1,0:T(8,128)(2,1)} async-done(((bf16[1,448,256]{2,1,0:T(8,128)(2,1)}), bf16[1,7168,256]{2,1,0:T(8,128)(2,1)}) %all-gather.15.cloned.1.call-update) | async-done | bytes 3670032 | tf_op jit(solution)/shard_map/all_gather | solution.py:68
  448.9 3.1 slice.46
  452.0 77.7 %reduce-scatter.10.cloned.1.call-done = f32[64,256]{1,0:T(8,128)} async-done(((f32[1024,256]{1,0:T(8,128)}), f32[64,256]{1,0:T(8,128)}) %reduce-scatter.10.cloned.1.call-update) | async-done | bytes 65552 | tf_op jit(solution)/shard_map/reduce_scatter | solution.py:99
  530.6 3.6 fusion.4
  538.3 3.4 fusion
  542.7 71.2 %reduce-scatter.12.cloned.1.call-done = f32[192,256]{1,0:T(8,128)} async-done(((f32[3072,256]{1,0:T(8,128)}), f32[192,256]{1,0:T(8,128)}) %reduce-scatter.12.cloned.1.call-update) | async-done | bytes 196624 | tf_op jit(solution)/shard_map/reduce_scatter | solution.py:92
  613.9 2.6 fusion.19
  622.0 75.1 %reduce-scatter.14.cloned.1.call-done = f32[32,256]{1,0:T(8,128)} async-done(((f32[512,256]{1,0:T(8,128)}), f32[32,256]{1,0:T(8,128)}) %reduce-scatter.14.cloned.1.call-update) | async-done | bytes 32784 | tf_op jit(solution)/shard_map/reduce_scatter | solution.py:99
  (88 shorter events, 47.3 us)
Async XLA Ops:
  7.2 46.5 %all-gather.9.cloned.1.call-start = ((), (), s32[]{:S(2)}) async-start(), calls=%async_computation.10 | async-start | bytes 2228224 | tf_op jit(solution)/shard_map/all_gather | solution.py:61
  7.9 97.0 %all-gather.11.cloned.1.call-start = ((), (), s32[]{:S(2)}) async-start(), calls=%async_computation.11 | async-start | bytes 2228224 | tf_op jit(solution)/shard_map/all_gather | solution.py:68
  8.6 246.8 %reduce-scatter.6.cloned.1.call-start = ((), (), s32[]{:S(2)}) async-start(), calls=%async_computation.5 | async-start | bytes 2228224 | tf_op jit(solution)/shard_map/reduce_scatter | solution.py:99
  108.1 1.6 collective-permute-start
  109.8 14.1 %collective-permute-start.1 = (f32[256,512]{0,1:T(8,128)S(1)}, f32[256,512]{0,1:T(8,128)S(1)}, u32[]{:S(2)}, u32[]{:S(2)}) collective-permute-start(f32[256,512]{0,1:T(8,128)S(1)} %maximum_select_fusion.7), channel_id=1, source_target_pairs={{0,2},{1,3},{2,0},{3,1},{4,6},{5,7},{6,4},{7,5},{8,10},{9,11},{10,... | collective-permute-start | bytes 1572872 | tf_op jit(solution)/shard_map/ppermute | solution.py:16
  123.9 47.9 %collective-permute-start.2 = (f32[256,1024]{0,1:T(8,128)S(1)}, f32[256,1024]{0,1:T(8,128)}, u32[]{:S(2)}, u32[]{:S(2)}) collective-permute-start(f32[256,1024]{0,1:T(8,128)S(1)} %maximum_select_fusion.2), channel_id=1, source_target_pairs={{0,4},{1,5},{2,6},{3,7},{4,0},{5,1},{6,2},{7,3},{8,12},{9,13},{10,... | collective-permute-start | bytes 3145736 | tf_op jit(solution)/shard_map/ppermute | solution.py:16
  126.5 47.2 %copy-start.9 = (bf16[1,256,256]{2,1,0:T(8,128)(2,1)S(1)}, bf16[1,256,256]{2,1,0:T(8,128)(2,1)}, u32[]{:S(2)}) copy-start(bf16[1,256,256]{2,1,0:T(8,128)(2,1)} %param.8) | copy-start | bytes 393220
  176.4 133.6 %all-gather.13.cloned.1.call-start = ((), (), s32[]{:S(2)}) async-start(), calls=%async_computation.12 | async-start | bytes 3342336 | tf_op jit(solution)/shard_map/all_gather | solution.py:68
  177.0 215.6 %reduce-scatter.8.cloned.1.call-start = ((), (), s32[]{:S(2)}) async-start(), calls=%async_computation.6 | async-start | bytes 2228224 | tf_op jit(solution)/shard_map/reduce_scatter | solution.py:92
  179.7 269.2 %all-gather.15.cloned.1.call-start = ((), (), s32[]{:S(2)}) async-start(), calls=%async_computation.13 | async-start | bytes 3899392 | tf_op jit(solution)/shard_map/all_gather | solution.py:68
  180.3 349.4 %reduce-scatter.10.cloned.1.call-start = ((), (), s32[]{:S(2)}) async-start(), calls=%async_computation.7 | async-start | bytes 1114112 | tf_op jit(solution)/shard_map/reduce_scatter | solution.py:99
  256.3 1.4 collective-permute-start.3
  257.8 8.4 %collective-permute-start.4 = (f32[128,512]{0,1:T(8,128)S(1)}, f32[128,512]{0,1:T(8,128)S(1)}, u32[]{:S(2)}, u32[]{:S(2)}) collective-permute-start(f32[128,512]{0,1:T(8,128)S(1)} %maximum_select_fusion.9), channel_id=1, source_target_pairs={{0,2},{1,3},{2,0},{3,1},{4,6},{5,7},{6,4},{7,5},{8,10},{9,11},{10,... | collective-permute-start | bytes 786440 | tf_op jit(solution)/shard_map/ppermute | solution.py:16
  266.3 48.7 %collective-permute-start.5 = (f32[128,1024]{0,1:T(8,128)S(1)}, f32[128,1024]{0,1:T(8,128)}, u32[]{:S(2)}, u32[]{:S(2)}) collective-permute-start(f32[128,1024]{0,1:T(8,128)S(1)} %maximum_select_fusion.8), channel_id=1, source_target_pairs={{0,4},{1,5},{2,6},{3,7},{4,0},{5,1},{6,2},{7,3},{8,12},{9,13},{10,... | collective-permute-start | bytes 1572872 | tf_op jit(solution)/shard_map/ppermute | solution.py:16
  396.8 1.8 collective-permute-start.6
  398.7 19.9 %collective-permute-start.7 = (f32[384,512]{1,0:T(8,128)S(1)}, f32[384,512]{1,0:T(8,128)S(1)}, u32[]{:S(2)}, u32[]{:S(2)}) collective-permute-start(f32[384,512]{1,0:T(8,128)S(1)} %maximum_select_fusion.6), channel_id=1, source_target_pairs={{0,2},{1,3},{2,0},{3,1},{4,6},{5,7},{6,4},{7,5},{8,10},{9,11},{10,... | collective-permute-start | bytes 2359304 | tf_op jit(solution)/shard_map/ppermute | solution.py:16
  422.4 191.5 %reduce-scatter.12.cloned.1.call-start = ((), (), s32[]{:S(2)}) async-start(), calls=%async_computation.8 | async-start | bytes 3342336 | tf_op jit(solution)/shard_map/reduce_scatter | solution.py:92
  432.5 264.6 %reduce-scatter.14.cloned.1.call-start = ((), (), s32[]{:S(2)}) async-start(), calls=%async_computation.9 | async-start | bytes 557056 | tf_op jit(solution)/shard_map/reduce_scatter | solution.py:99
  448.9 80.8 %copy-start.11 = (bf16[1,64,256]{2,1,0:T(8,128)(2,1)S(1)}, bf16[1,64,256]{2,1,0:T(8,128)(2,1)}, u32[]{:S(2)}) copy-start(bf16[1,64,256]{2,1,0:T(8,128)(2,1)} %param.11) | copy-start | bytes 98308
  530.5 6.1 collective-permute-start.8
  536.7 6.0 collective-permute-start.9
  541.7 76.7 %copy-start.7 = (bf16[1,448,256]{2,1,0:T(8,128)(2,1)S(1)}, bf16[1,448,256]{2,1,0:T(8,128)(2,1)}, u32[]{:S(2)}) copy-start(bf16[1,448,256]{2,1,0:T(8,128)(2,1)} %param.12) | copy-start | bytes 688132
  616.5 80.6 %copy-start.12 = (bf16[1,32,256]{2,1,0:T(8,128)(2,1)S(1)}, bf16[1,32,256]{2,1,0:T(8,128)(2,1)}, u32[]{:S(2)}) copy-start(bf16[1,32,256]{2,1,0:T(8,128)(2,1)} %param.13) | copy-start | bytes 49156
  616.5 1.9 collective-permute-start.10
  (9 other events, 41.3 us)
Sparse Core Ops, SparseCore 0:
  9.8 43.8 all-gather.8
  56.1 48.7 all-gather.10
  176.5 78.8 reduce-scatter.5
  258.1 51.9 all-gather.12
  313.8 78.7 reduce-scatter.7
  394.9 53.9 all-gather.14
  452.4 77.2 reduce-scatter.9
  533.8 80.1 reduce-scatter.11
  620.4 76.6 reduce-scatter.13
where the time goes:
time: 706 us; the launch traced here: 705 us
  waiting for transfers between devices  620 us (88%)
  matrix products  31.8 us (5%)
  local copies, waits for them, and re-layouts  15.5 us (2%)
  between operations  14.1 us (2%)
  starting transfers between devices  12.7 us (2%)
  other arithmetic  10.9 us (2%)
    reduce_scatter x3, waiting for transfers between devices, per_device(): lax.psum_scatter(diag_terms, 'row', scatter_dimension=0, tiled=True)  228 us
    reduce_scatter x2, waiting for transfers between devices, per_device(): reduced = lax.psum_scatter(joined, 'row', scatter_dimension=0, tiled=True)  147 us
    all_gather x3, waiting for transfers between devices, per_device(): gathered = lax.all_gather(factor_tile, 'row', axis=0, tiled=True)  109 us
    ppermute x11, waiting for transfers between devices, swapped(): return lax.ppermute(value, axis, pairs)  89.8 us
    all_gather x1, waiting for transfers between devices, per_device(): root_rows = lax.all_gather(root_block[0], 'col', axis=1, tiled=True)  45 us
    dot_general x6, matrix products, transposed_product(): lax.dot_general(left_side, right_side, (((0,), (0,)), ((), ())), precisio...  14.2 us
  transfers between devices with their start and end apart: 20, of which 18 were waited for; matrix products, arithmetic and copies ran while one was open for 6% of the time, Pallas kernels for 0%

commit v1 on v0

--- a/solution.py
+++ b/solution.py
@@ -8,6 +8,24 @@
 S2 = 1024
 S3 = 512
 exact_mode = lax.Precision.HIGHEST
+
+
+def gather_around(array, axis, dim):
+    ways, here, step = (lax.axis_size(axis), lax.axis_index(axis), array.shape[dim])
+    dims = [n * ways if d == dim else n for d, n in enumerate(array.shape)]
+    full = lax.dynamic_update_slice_in_dim(
+        jnp.zeros(dims, array.dtype), array, here * step, axis=dim
+    )
+    going_up = going_down = array
+    for far in range(1, ways // 2 + 1):
+        going_up = lax.ppermute(going_up, axis, [(d, (d + 1) % ways) for d in range(ways)])
+        full = lax.dynamic_update_slice_in_dim(full, going_up, (here - far) % ways * step, axis=dim)
+        if 2 * far < ways:
+            going_down = lax.ppermute(going_down, axis, [(d, (d - 1) % ways) for d in range(ways)])
+            full = lax.dynamic_update_slice_in_dim(
+                full, going_down, (here + far) % ways * step, axis=dim
+            )
+    return full
 
 
 def swapped(value, axis, apart):
@@ -58,7 +76,7 @@
     ]
     factors = [l_one[0], l_two[0], l_three[0]]
     inverses = [dinv_one[0], dinv_two[0], dinv_three[0]]
-    root_rows = lax.all_gather(root_block[0], "col", axis=1, tiled=True)
+    root_rows = gather_around(root_block[0], "col", 1)
     panels = [root_rows]
     crossed = [root_rows]
     outputs = []

time: 706 us -> 664 us (0.941)
  waiting for transfers between devices: 620 us -> 554 us
  starting transfers between devices: 12.7 us -> 36.1 us
    all_gather x1 -> x0, waiting for transfers between devices: 45 us -> none  [per_device(): root_rows = lax.all_gather(root_block[0], 'col', axis=1, tiled=True)]
    all_gather x3, waiting for transfers between devices: 109 us -> 65.1 us  [per_device(): gathered = lax.all_gather(factor_tile, 'row', axis=0, tiled=True)]
    ppermute x0 -> x15, waiting for transfers between devices: none -> 23.7 us  [the longest x8 23.6 us: gather_around(): lax.ppermute(going_up, axis, [(d, (d + 1) % ways) for d in range(ways)])]
    ppermute x0 -> x15, starting transfers between devices: none -> 23.2 us  [the longest x7 23.1 us: gather_around(): lax.ppermute(going_down, axis, [(d, (d - 1) % ways) for d in range(ways)])]
  transfers between devices with their start and end apart: 20 -> 34, of which waited for: 18 -> 25; matrix products, arithmetic and copies ran while one was open for 6% -> 7% of each run, Pallas kernels for 0% -> 0%
where the time goes in v1:
time: 664 us; the launch traced here: 663 us
  waiting for transfers between devices  554 us (83%)
  starting transfers between devices  36.1 us (5%)
  matrix products  31.3 us (5%)
  local copies, waits for them, and re-layouts  15.9 us (2%)
  between operations  14.6 us (2%)
  other arithmetic  10.8 us (2%)
    reduce_scatter x3, waiting for transfers between devices, per_device(): lax.psum_scatter(diag_terms, 'row', scatter_dimension=0, tiled=True)  227 us
    reduce_scatter x2, waiting for transfers between devices, per_device(): reduced = lax.psum_scatter(joined, 'row', scatter_dimension=0, tiled=True)  146 us
    ppermute x11, waiting for transfers between devices, swapped(): return lax.ppermute(value, axis, pairs)  89.8 us
    all_gather x3, waiting for transfers between devices, per_device(): gathered = lax.all_gather(factor_tile, 'row', axis=0, tiled=True)  65.1 us
    ppermute x8, waiting for transfers between devices, gather_around(): lax.ppermute(going_up, axis, [(d, (d + 1) % ways) for d in range(ways)])  23.6 us
    ppermute x7, starting transfers between devices, gather_around(): lax.ppermute(going_down, axis, [(d, (d - 1) % ways) for d in range(ways)])  23.1 us
    dot_general x6, matrix products, transposed_product(): lax.dot_general(left_side, right_side, (((0,), (0,)), ((), ())), precisio...  14.3 us
  transfers between devices with their start and end apart: 34, of which 25 were waited for; matrix products, arithmetic and copies ran while one was open for 7% of the time, Pallas kernels for 0%

profile of v1, /device:TPU:2, one launch (start us, length us, event | category | flops | bytes accessed | tf_op | source)
XLA Modules:
  0.0 663.0 jit_solution(10453292245834233778)
XLA Ops:
  8.0 5.3 collective-permute-start.1
  16.1 3.0 collective-permute-start.3
  21.7 3.0 collective-permute-start.5
  27.3 3.0 collective-permute-start.7
  32.9 3.0 collective-permute-start.9
  44.2 3.0 collective-permute-start.13
  49.8 5.5 collective-permute-done.14
  55.4 7.7 %all-gather.7.cloned.1.call-done = bf16[1,4096,256]{2,1,0:T(8,128)(2,1)} async-done(((bf16[1,256,256]{2,1,0:T(8,128)(2,1)}), bf16[1,4096,256]{2,1,0:T(8,128)(2,1)}) %all-gather.7.cloned.1.call-update) | async-done | bytes 2097168 | tf_op jit(solution)/shard_map/all_gather | solution.py:86
  68.9 12.4 %collective-permute-done.16 = f32[256,512]{0,1:T(8,128)S(1)} collective-permute-done((f32[256,512]{0,1:T(8,128)S(1)}, f32[256,512]{0,1:T(8,128)S(1)}, u32[]{:S(2)}, u32[]{:S(2)}) %collective-permute-start.16) | collective-permute-done | bytes 524320 | tf_op jit(solution)/shard_map/ppermute | solution.py:34
  84.0 45.3 %collective-permute-done.17 = f32[256,1024]{0,1:T(8,128)} collective-permute-done((f32[256,1024]{0,1:T(8,128)S(1)}, f32[256,1024]{0,1:T(8,128)}, u32[]{:S(2)}, u32[]{:S(2)}) %collective-permute-start.17) | collective-permute-done | bytes 1048608 | tf_op jit(solution)/shard_map/ppermute | solution.py:34
  138.1 74.7 %reduce-scatter.6.cloned.1.call-done = f32[128,256]{0,1:T(8,128)} async-done(((f32[2048,256]{0,1:T(8,128)}), f32[128,256]{0,1:T(8,128)}) %reduce-scatter.6.cloned.1.call-update) | async-done | bytes 131088 | tf_op jit(solution)/shard_map/reduce_scatter | solution.py:117
  216.8 6.8 %collective-permute-done.19 = f32[128,512]{0,1:T(8,128)S(1)} collective-permute-done((f32[128,512]{0,1:T(8,128)S(1)}, f32[128,512]{0,1:T(8,128)S(1)}, u32[]{:S(2)}, u32[]{:S(2)}) %collective-permute-start.19) | collective-permute-done | bytes 262176 | tf_op jit(solution)/shard_map/ppermute | solution.py:34
  226.5 41.0 %all-gather.9.cloned.1.call-done = bf16[1,6144,256]{2,1,0:T(8,128)(2,1)} async-done(((bf16[1,384,256]{2,1,0:T(8,128)(2,1)}), bf16[1,6144,256]{2,1,0:T(8,128)(2,1)}) %all-gather.9.cloned.1.call-update) | async-done | bytes 3145744 | tf_op jit(solution)/shard_map/all_gather | solution.py:86
  274.8 75.3 %reduce-scatter.8.cloned.1.call-done = f32[128,256]{1,0:T(8,128)} async-done(((f32[2048,256]{1,0:T(8,128)}), f32[128,256]{1,0:T(8,128)}) %reduce-scatter.8.cloned.1.call-update) | async-done | bytes 131088 | tf_op jit(solution)/shard_map/reduce_scatter | solution.py:110
  350.1 4.2 add_negate_fusion.1
  357.8 18.0 %collective-permute-done.22 = f32[384,512]{1,0:T(8,128)S(1)} collective-permute-done((f32[384,512]{1,0:T(8,128)S(1)}, f32[384,512]{1,0:T(8,128)S(1)}, u32[]{:S(2)}, u32[]{:S(2)}) %collective-permute-start.22) | collective-permute-done | bytes 786464 | tf_op jit(solution)/shard_map/ppermute | solution.py:34
  382.3 3.0 copy.16
  389.9 16.4 %all-gather.11.cloned.1.call-done = bf16[1,7168,256]{2,1,0:T(8,128)(2,1)} async-done(((bf16[1,448,256]{2,1,0:T(8,128)(2,1)}), bf16[1,7168,256]{2,1,0:T(8,128)(2,1)}) %all-gather.11.cloned.1.call-update) | async-done | bytes 3670032 | tf_op jit(solution)/shard_map/all_gather | solution.py:86
  406.3 3.1 slice.46
  409.4 77.6 %reduce-scatter.10.cloned.1.call-done = f32[64,256]{1,0:T(8,128)} async-done(((f32[1024,256]{1,0:T(8,128)}), f32[64,256]{1,0:T(8,128)}) %reduce-scatter.10.cloned.1.call-update) | async-done | bytes 65552 | tf_op jit(solution)/shard_map/reduce_scatter | solution.py:117
  487.9 3.6 fusion.39
  495.9 3.4 fusion
  500.3 71.1 %reduce-scatter.12.cloned.1.call-done = f32[192,256]{1,0:T(8,128)} async-done(((f32[3072,256]{1,0:T(8,128)}), f32[192,256]{1,0:T(8,128)}) %reduce-scatter.12.cloned.1.call-update) | async-done | bytes 196624 | tf_op jit(solution)/shard_map/reduce_scatter | solution.py:110
  579.5 75.1 %reduce-scatter.14.cloned.1.call-done = f32[32,256]{1,0:T(8,128)} async-done(((f32[512,256]{1,0:T(8,128)}), f32[32,256]{1,0:T(8,128)}) %reduce-scatter.14.cloned.1.call-update) | async-done | bytes 32784 | tf_op jit(solution)/shard_map/reduce_scatter | solution.py:117
  (136 shorter events, 84.0 us)
Async XLA Ops:
  7.2 55.9 %all-gather.7.cloned.1.call-start = ((), (), s32[]{:S(2)}) async-start(), calls=%async_computation.10 | async-start | bytes 2228224 | tf_op jit(solution)/shard_map/all_gather | solution.py:86
  7.9 204.9 %reduce-scatter.6.cloned.1.call-start = ((), (), s32[]{:S(2)}) async-start(), calls=%async_computation.5 | async-start | bytes 2228224 | tf_op jit(solution)/shard_map/reduce_scatter | solution.py:117
  8.0 8.2 %collective-permute-start = (bf16[256,256]{1,0:T(8,128)(2,1)}, bf16[256,256]{1,0:T(8,128)(2,1)S(1)}, u32[]{:S(2)}, u32[]{:S(2)}) collective-permute-start(bf16[256,256]{1,0:T(8,128)(2,1)} %bitcast.82), channel_id=1, source_target_pairs={{0,1},{1,2},{2,3},{3,4},{4,5},{5,6},{6,7},{7,8},{8,9},{9,10},{10,1... | collective-permute-start | bytes 393224 | tf_op jit(solution)/shard_map/ppermute | solution.py:21
  8.0 8.2 %collective-permute-start.1 = (bf16[256,256]{1,0:T(8,128)(2,1)}, bf16[256,256]{1,0:T(8,128)(2,1)S(1)}, u32[]{:S(2)}, u32[]{:S(2)}) collective-permute-start(bf16[256,256]{1,0:T(8,128)(2,1)} %bitcast.83), channel_id=1, source_target_pairs={{0,15},{1,0},{2,1},{3,2},{4,3},{5,4},{6,5},{7,6},{8,7},{9,8},{10,9... | collective-permute-start | bytes 393224 | tf_op jit(solution)/shard_map/ppermute | solution.py:24
  16.1 5.6 collective-permute-start.2
  16.1 5.6 collective-permute-start.3
  21.7 5.6 collective-permute-start.4
  21.7 5.6 collective-permute-start.5
  32.9 5.6 collective-permute-start.8
  44.1 5.6 collective-permute-start.12
  44.2 5.6 collective-permute-start.13
  67.3 14.1 %collective-permute-start.16 = (f32[256,512]{0,1:T(8,128)S(1)}, f32[256,512]{0,1:T(8,128)S(1)}, u32[]{:S(2)}, u32[]{:S(2)}) collective-permute-start(f32[256,512]{0,1:T(8,128)S(1)} %maximum_select_fusion.7), channel_id=1, source_target_pairs={{0,2},{1,3},{2,0},{3,1},{4,6},{5,7},{6,4},{7,5},{8,10},{9,11},{10,... | collective-permute-start | bytes 1572872 | tf_op jit(solution)/shard_map/ppermute | solution.py:34
  81.4 47.9 %collective-permute-start.17 = (f32[256,1024]{0,1:T(8,128)S(1)}, f32[256,1024]{0,1:T(8,128)}, u32[]{:S(2)}, u32[]{:S(2)}) collective-permute-start(f32[256,1024]{0,1:T(8,128)S(1)} %maximum_select_fusion.2), channel_id=1, source_target_pairs={{0,4},{1,5},{2,6},{3,7},{4,0},{5,1},{6,2},{7,3},{8,12},{9,13},{10,... | collective-permute-start | bytes 3145736 | tf_op jit(solution)/shard_map/ppermute | solution.py:34
  133.8 133.6 %all-gather.9.cloned.1.call-start = ((), (), s32[]{:S(2)}) async-start(), calls=%async_computation.11 | async-start | bytes 3342336 | tf_op jit(solution)/shard_map/all_gather | solution.py:86
  134.6 215.5 %reduce-scatter.8.cloned.1.call-start = ((), (), s32[]{:S(2)}) async-start(), calls=%async_computation.6 | async-start | bytes 2228224 | tf_op jit(solution)/shard_map/reduce_scatter | solution.py:110
  137.2 269.2 %all-gather.11.cloned.1.call-start = ((), (), s32[]{:S(2)}) async-start(), calls=%async_computation.12 | async-start | bytes 3899392 | tf_op jit(solution)/shard_map/all_gather | solution.py:86
  137.8 349.3 %reduce-scatter.10.cloned.1.call-start = ((), (), s32[]{:S(2)}) async-start(), calls=%async_computation.7 | async-start | bytes 1114112 | tf_op jit(solution)/shard_map/reduce_scatter | solution.py:117
  215.2 8.4 %collective-permute-start.19 = (f32[128,512]{0,1:T(8,128)S(1)}, f32[128,512]{0,1:T(8,128)S(1)}, u32[]{:S(2)}, u32[]{:S(2)}) collective-permute-start(f32[128,512]{0,1:T(8,128)S(1)} %maximum_select_fusion.9), channel_id=1, source_target_pairs={{0,2},{1,3},{2,0},{3,1},{4,6},{5,7},{6,4},{7,5},{8,10},{9,11},{10,... | collective-permute-start | bytes 786440 | tf_op jit(solution)/shard_map/ppermute | solution.py:34
  223.7 48.8 %collective-permute-start.20 = (f32[128,1024]{0,1:T(8,128)S(1)}, f32[128,1024]{0,1:T(8,128)}, u32[]{:S(2)}, u32[]{:S(2)}) collective-permute-start(f32[128,1024]{0,1:T(8,128)S(1)} %maximum_select_fusion.8), channel_id=1, source_target_pairs={{0,4},{1,5},{2,6},{3,7},{4,0},{5,1},{6,2},{7,3},{8,12},{9,13},{10,... | collective-permute-start | bytes 1572872 | tf_op jit(solution)/shard_map/ppermute | solution.py:34
  356.1 19.7 %collective-permute-start.22 = (f32[384,512]{1,0:T(8,128)S(1)}, f32[384,512]{1,0:T(8,128)S(1)}, u32[]{:S(2)}, u32[]{:S(2)}) collective-permute-start(f32[384,512]{1,0:T(8,128)S(1)} %maximum_select_fusion.6), channel_id=1, source_target_pairs={{0,2},{1,3},{2,0},{3,1},{4,6},{5,7},{6,4},{7,5},{8,10},{9,11},{10,... | collective-permute-start | bytes 2359304 | tf_op jit(solution)/shard_map/ppermute | solution.py:34
  379.8 191.6 %reduce-scatter.12.cloned.1.call-start = ((), (), s32[]{:S(2)}) async-start(), calls=%async_computation.8 | async-start | bytes 3342336 | tf_op jit(solution)/shard_map/reduce_scatter | solution.py:110
  389.9 264.7 %reduce-scatter.14.cloned.1.call-start = ((), (), s32[]{:S(2)}) async-start(), calls=%async_computation.9 | async-start | bytes 557056 | tf_op jit(solution)/shard_map/reduce_scatter | solution.py:117
  487.9 6.1 collective-permute-start.23
  494.0 6.2 collective-permute-start.24
  (25 other events, 383.4 us)
Sparse Core Ops, SparseCore 0:
  10.4 52.5 all-gather.6
  134.0 78.7 reduce-scatter.5
  215.6 51.8 all-gather.8
  271.3 78.7 reduce-scatter.7
  352.4 53.8 all-gather.10
  409.7 77.3 reduce-scatter.9
  491.1 80.2 reduce-scatter.11
  577.8 76.6 reduce-scatter.13
